TPU v7x, 32 devices: a whole 2x2x4 slice. The times are simulated.
32 devices in a mesh: groups: 2 (over x), bricks: 16 (over z, y, core).
Axes of the slice: x: 2, y: 2, z: 4, core: 2. Of those that a mesh axis runs over, the one named last changes fastest.
Arguments:
- snapshots: bfloat16 [512, 32, 32, 256], P(('groups', 'bricks')), parts along dimension 0, may hold values from -30 to 30
- material: int32 [512, 1024], P(('groups', 'bricks')), parts along dimension 0, may hold values from 0 to 15
- occupancy: int32 [32, 4], P(('groups', 'bricks')), parts along dimension 0, may hold values 0 or 1
- moduli: bfloat16 [16], replicated, may hold values from 0.19921875 to 5
Outputs:
- energy_gram: float32 [512, 256], P(('groups', 'bricks')), parts along dimension 0
There are 2 independent parts, one for each index of `groups`. A program takes and returns all parts, laid end to end along the dimension named above; an argument that names none is the same for every part. Nothing has to cross between parts.
All inputs are finite; a program needn't handle non-finite values. No bound on the sum of `occupancy` on one device may be relied on, other than what follows from the above.
Results may differ from a plain program's by a relative error of at most 0.0003.
Values may be sent and summed in bfloat16 or wider, within the bound.
No kernel may reach another device: no remote copies, remote signals or barrier semaphores. Data moves between devices by JAX's collectives and lax.ppermute only.
A program may use at most 128 MiB of HBM per device.

v0:
```python
import jax
import jax.numpy as jnp
from jax import lax
from jax.sharding import PartitionSpec as P


def with_halo(block, sides, width):
    for axis, dim in sides:
        count = lax.axis_size(axis)
        forward = [(i, i + 1) for i in range(count - 1)]
        backward = [(target, source) for source, target in forward]
        low = lax.ppermute(
            lax.slice_in_dim(block, block.shape[dim] - width, None, axis=dim), axis, forward
        )
        high = lax.ppermute(lax.slice_in_dim(block, 0, width, axis=dim), axis, backward)
        block = jnp.concatenate([low, block, high], axis=dim)
    return block


def stencil(padded_field, padded_modulus):
    depth = padded_field.shape[0] - 2
    rows_y = padded_field.shape[1]
    rows_x = padded_field.shape[2]
    field_full = jnp.pad(padded_field, ((0, 0), (1, 1), (1, 1), (0, 0)))
    modulus_full = jnp.pad(padded_modulus, ((0, 0), (1, 1), (1, 1)))
    center = field_full[1 : 1 + depth, 1 : 1 + rows_y, 1 : 1 + rows_x]
    center_mod = modulus_full[1 : 1 + depth, 1 : 1 + rows_y, 1 : 1 + rows_x]
    mod_sum = jnp.zeros_like(center_mod)
    field_sum = jnp.zeros_like(center)
    product_sum = jnp.zeros_like(center)
    total_weight = 0.0
    for shift_z in (-1, 0, 1):
        for shift_y in (-1, 0, 1):
            for shift_x in (-1, 0, 1):
                nonzero = abs(shift_z) + abs(shift_y) + abs(shift_x)
                if nonzero == 0:
                    continue
                weight = (1.0, 0.5, 0.25)[nonzero - 1]
                total_weight = total_weight + weight
                near = field_full[
                    1 + shift_z : 1 + shift_z + depth,
                    1 + shift_y : 1 + shift_y + rows_y,
                    1 + shift_x : 1 + shift_x + rows_x,
                ]
                near_mod = modulus_full[
                    1 + shift_z : 1 + shift_z + depth,
                    1 + shift_y : 1 + shift_y + rows_y,
                    1 + shift_x : 1 + shift_x + rows_x,
                ]
                mod_sum = mod_sum + weight * near_mod
                field_sum = field_sum + weight * near
                product_sum = product_sum + weight * near_mod[..., None] * near
    diagonal = 0.5 * (total_weight * center_mod + mod_sum)
    return (
        diagonal[..., None] * center - 0.5 * center_mod[..., None] * field_sum - 0.5 * product_sum
    )


def local(snapshots, material, occupancy, moduli):
    depth, rows_y, rows_x, width = snapshots.shape
    owners = lax.axis_size("bricks")
    tiles = occupancy.reshape(rows_y // 16, rows_x // 16)
    occupied = jnp.repeat(jnp.repeat(tiles, 16, 0), 16, 1).astype(jnp.bfloat16)
    classes = jnp.arange(moduli.shape[0], dtype=jnp.int32)
    matches = material[..., None] == classes
    looked = jnp.sum(jnp.where(matches, moduli.astype(jnp.float32), 0.0), axis=-1)
    modulus = looked.astype(jnp.bfloat16).reshape(depth, rows_y, rows_x) * occupied[None]
    field = snapshots * occupied[None, :, :, None]
    padded_field, padded_modulus = (
        with_halo(field, (("bricks", 0),), 1),
        with_halo(modulus, (("bricks", 0),), 1),
    )
    image = stencil(padded_field.astype(jnp.float32), padded_modulus.astype(jnp.float32)).astype(
        jnp.bfloat16
    )
    field_flat = field.reshape(-1, width)
    image_flat = image.reshape(-1, width)
    scale = 1.0 / (depth * rows_y * rows_x * owners)
    own_rows = width // owners
    local_gram = lax.dot_general(
        field_flat, image_flat, (((0,), (0,)), ((), ())), preferred_element_type=jnp.float32
    )
    summed = lax.psum(local_gram, "bricks")
    start = lax.axis_index("bricks") * own_rows
    result = lax.dynamic_slice_in_dim(summed, start, own_rows, 0)
    return result * scale


def solution(mesh):
    in_specs = (
        P(("groups", "bricks"), None, None, None),
        P(("groups", "bricks"), None),
        P(("groups", "bricks"), None),
        P(),
    )
    out_specs = P(("groups", "bricks"), None)
    return jax.shard_map(local, mesh=mesh, in_specs=in_specs, out_specs=out_specs, check_vma=False)
```

profile of v0, /device:TPU:1, one launch (start us, length us, event | category | flops | bytes accessed | tf_op | source)
XLA Modules:
  0.0 343.4 jit_solution(14337007187639578546)
XLA Ops:
  6.5 0.7 convert_reduce_fusion
  7.2 0.1 convert_element_type.46
  7.3 0.1 copy.10
  7.4 0.1 broadcast_in_dim.12
  7.5 0.1 convert_element_type.47
  7.6 0.1 copy.11
  7.7 0.7 convert_element_type.49
  8.3 1.1 select_reduce_fusion
  9.5 0.1 convert_element_type.51
  9.7 4.5 %collective-permute-start = (bf16[1,32,32]{2,1,0:T(8,128)(2,1)S(1)}, bf16[1,32,32]{2,1,0:T(8,128)(2,1)S(1)}, u32[]{:S(2)}, u32[]{:S(2)}) collective-permute-start(bf16[1,32,32]{2,1,0:T(8,128)(2,1)S(1)} %get-tuple-element.35), channel_id=1, source_target_pairs={{0,1},{1,2},{2,3},{3,4},{4,5},{5,6},{6,7},{7,8},{8,9},{9,10},{10,1... | collective-permute-start | bytes 6152 | tf_op jit(solution)/shard_map/ppermute | solution.py:12
  14.2 1.9 collective-permute-start.1
  16.1 8.0 %broadcast_multiply_fusion = bf16[16,32,32,256]{3,2,1,0:T(8,128)(2,1)} fusion(bf16[16,32,32,256]{3,2,1,0:T(8,128)(2,1)} %param.4, bf16[32,32]{1,0:T(8,128)(2,1)S(1)} %copy.11), kind=kLoop, calls=%fused_computation.30 | loop fusion | flops 4194304 | bytes 16779264 | tf_op jit(solution)/shard_map/mul | solution.py:68
  24.2 1.3 fusion.31
  25.4 3.6 %collective-permute-start.2 = (bf16[1,32,32,256]{3,2,1,0:T(8,128)(2,1)S(1)}, bf16[1,32,32,256]{3,2,1,0:T(8,128)(2,1)S(1)}, u32[]{:S(2)}, u32[]{:S(2)}) collective-permute-start(bf16[1,32,32,256]{3,2,1,0:T(8,128)(2,1)S(1)} %get-tuple-element.5), channel_id=1, source_target_pairs={{0,1},{1,2},{2,3},{3,4},{4,5},{5,6},{6,7},{7,8},{8,9},{9,10},{10,1... | collective-permute-start | bytes 1572872 | tf_op jit(solution)/shard_map/ppermute | solution.py:12
  29.1 1.9 collective-permute-start.3
  31.1 2.3 fusion.8
  33.4 3.5 %add_multiply_fusion = (f32[16,32,32]{2,1,0:T(8,128)S(1)}, f32[16,32,32]{2,1,0:T(8,128)S(1)}, f32[16,32,32]{2,1,0:T(8,128)S(1)}, f32[16,32,32]{2,1,0:T(8,128)S(1...) fusion(f32[18,32,32]{2,1,0:T(8,128)S(1)} %maximum_convert_fusion.1), kind=kLoop, calls=%fused_computation.78 | loop fusion | flops 966656 | bytes 2129920 | tf_op jit(solution)/shard_map/mul | solution.py:53
  36.9 2.6 collective-permute-done.3
  39.6 11.4 %maximum_convert_fusion = f32[18,32,32,256]{3,2,1,0:T(8,128)} fusion(bf16[1,32,32,256]{3,2,1,0:T(8,128)(2,1)S(1)} %collective-permute-done.3, bf16[16,32,32,256]{3,2,1,0:T(8,128)(2,1)} %broadcast_multiply_fusion, bf16[1,32,32,256]{3,2,1,0:T(8,128)(2,1)S(1)} %collective-permute-done.2), kind=kLoop, calls=%fused_computation.28 | loop fusion | flops 14155776 | bytes 28311552 | tf_op jit(solution)/shard_map/convert_element_type | solution.py:73
  51.0 184.7 %fusion.37 = bf16[16,32,32,256]{3,2,1,0:T(8,128)(2,1)S(1)} fusion(f32[18,32,32,256]{3,2,1,0:T(8,128)} %maximum_convert_fusion, f32[16,32,32]{2,1,0:T(8,128)} %get-tuple-element.32, f32[16,32,32]{2,1,0:T(8,128)} %get-tuple-element.31, f32[16,32,32]{2,1,0:T(8,128)} %get-tuple-element.30, f32[16,32,32]{2,1,0:T(8,128)} %get-tuple-element.29, ...), kind=kLoop, calls=%fused_computation.27.clone.clone.clone.clone.1 | loop fusion | flops 427819008 | bytes 83951616 | tf_op jit(solution)/shard_map/dot_general | solution.py:80
  235.7 6.5 %fusion.5 = f32[256,256]{1,0:T(8,128)} fusion(bf16[16,32,32,256]{3,2,1,0:T(8,128)(2,1)} %broadcast_multiply_fusion, bf16[16,32,32,256]{3,2,1,0:T(8,128)(2,1)S(1)} %fusion.37), kind=kOutput, calls=%fused_computation.31 | convolution fusion | flops 2147483648 | bytes 17039360 | tf_op jit(solution)/shard_map/dot_general | solution.py:80
  242.1 0.0 all-reduce.4.cloned.1.call-update
  242.2 93.1 %all-reduce.4.cloned.1.call-done = f32[256,256]{1,0:T(8,128)} async-done(((f32[256,256]{1,0:T(8,128)}), f32[256,256]{1,0:T(8,128)}) %all-reduce.4.cloned.1.call-update) | async-done | bytes 262160 | tf_op jit(solution)/shard_map/psum | solution.py:83
  335.2 1.3 dynamic-slice_multiply_fusion
  (8 shorter events, 0.1 us)
Async XLA Ops:
  6.5 328.7 %all-reduce.4.cloned.1.call-start = ((), (), s32[]{:S(2)}) async-start(), calls=%async_computation | async-start | bytes 524288 | tf_op jit(solution)/shard_map/psum | solution.py:83
  9.7 21.4 %collective-permute-start = (bf16[1,32,32]{2,1,0:T(8,128)(2,1)S(1)}, bf16[1,32,32]{2,1,0:T(8,128)(2,1)S(1)}, u32[]{:S(2)}, u32[]{:S(2)}) collective-permute-start(bf16[1,32,32]{2,1,0:T(8,128)(2,1)S(1)} %get-tuple-element.35), channel_id=1, source_target_pairs={{0,1},{1,2},{2,3},{3,4},{4,5},{5,6},{6,7},{7,8},{8,9},{9,10},{10,1... | collective-permute-start | bytes 6152 | tf_op jit(solution)/shard_map/ppermute | solution.py:12
  14.2 16.8 %collective-permute-start.1 = (bf16[1,32,32]{2,1,0:T(8,128)(2,1)S(1)}, bf16[1,32,32]{2,1,0:T(8,128)(2,1)S(1)}, u32[]{:S(2)}, u32[]{:S(2)}) collective-permute-start(bf16[1,32,32]{2,1,0:T(8,128)(2,1)S(1)} %get-tuple-element.36), channel_id=1, source_target_pairs={{1,0},{2,1},{3,2},{4,3},{5,4},{6,5},{7,6},{8,7},{9,8},{10,9},{11,1... | collective-permute-start | bytes 6152 | tf_op jit(solution)/shard_map/ppermute | solution.py:15
  25.4 11.5 %collective-permute-start.2 = (bf16[1,32,32,256]{3,2,1,0:T(8,128)(2,1)S(1)}, bf16[1,32,32,256]{3,2,1,0:T(8,128)(2,1)S(1)}, u32[]{:S(2)}, u32[]{:S(2)}) collective-permute-start(bf16[1,32,32,256]{3,2,1,0:T(8,128)(2,1)S(1)} %get-tuple-element.5), channel_id=1, source_target_pairs={{0,1},{1,2},{2,3},{3,4},{4,5},{5,6},{6,7},{7,8},{8,9},{9,10},{10,1... | collective-permute-start | bytes 1572872 | tf_op jit(solution)/shard_map/ppermute | solution.py:12
  29.1 10.5 %collective-permute-start.3 = (bf16[1,32,32,256]{3,2,1,0:T(8,128)(2,1)S(1)}, bf16[1,32,32,256]{3,2,1,0:T(8,128)(2,1)S(1)}, u32[]{:S(2)}, u32[]{:S(2)}) collective-permute-start(bf16[1,32,32,256]{3,2,1,0:T(8,128)(2,1)S(1)} %get-tuple-element.6), channel_id=1, source_target_pairs={{1,0},{2,1},{3,2},{4,3},{5,4},{6,5},{7,6},{8,7},{9,8},{10,9},{11,1... | collective-permute-start | bytes 1572872 | tf_op jit(solution)/shard_map/ppermute | solution.py:15
Sparse Core Ops, SparseCore 0:
  242.3 92.8 all-reduce.3
where the time goes:
time: 344 us; the launch traced here: 343 us
  other arithmetic  214 us (62%)
  waiting for transfers between devices  95.7 us (28%)
  between operations  13.5 us (4%)
  starting transfers between devices  12 us (3%)
  matrix products  6.48 us (2%)
    dot_general x1, other arithmetic, local(): lax.dot_general(field_flat, image_flat, (((0,), (0,)), ((), ())), preferr...  185 us
    psum x1, waiting for transfers between devices, local(): summed = lax.psum(local_gram, 'bricks')  93.1 us
    convert_element_type x1, other arithmetic, local(): padded_field.astype(jnp.float32)  11.4 us
    ppermute x2, starting transfers between devices, with_halo(): lax.ppermute(lax.slice_in_dim(block, block.shape[dim] - width, None, axis...  8.18 us
    mul x1, other arithmetic, local(): field = snapshots * occupied[None, :, :, None]  8.04 us
  transfers between devices with their start and end apart: 5, of which 2 were waited for; matrix products, arithmetic and copies ran while one was open for 4% of the time, Pallas kernels for 0%

commit v1 on v0

--- a/solution.py
+++ b/solution.py
@@ -80,7 +80,9 @@
     local_gram = lax.dot_general(
         field_flat, image_flat, (((0,), (0,)), ((), ())), preferred_element_type=jnp.float32
     )
-    summed = lax.psum(local_gram, "bricks")
+    summed = local_gram
+    for hop in (1, 2, 4, 8):
+        summed = summed + lax.ppermute(summed, "bricks", [(dev, dev ^ hop) for dev in range(16)])
     start = lax.axis_index("bricks") * own_rows
     result = lax.dynamic_slice_in_dim(summed, start, own_rows, 0)
     return result * scale

time: 344 us -> 272 us (0.79)
  waiting for transfers between devices: 95.7 us -> 28.1 us
  between operations: 13.5 us -> 0.13 us
  starting transfers between devices: 12 us -> 20.6 us
    psum x1 -> x0, waiting for transfers between devices: 93.1 us -> none  [local(): summed = lax.psum(local_gram, 'bricks')]
    ppermute x0 -> x4, waiting for transfers between devices: none -> 25.4 us  [local(): lax.ppermute(summed, 'bricks', [(dev, dev ^ hop) for dev in range(16)])]
    ppermute x0 -> x4, starting transfers between devices: none -> 8.62 us  [local(): lax.ppermute(summed, 'bricks', [(dev, dev ^ hop) for dev in range(16)])]
  transfers between devices with their start and end apart: 5 -> 8, of which waited for: 2 -> 5; matrix products, arithmetic and copies ran while one was open for 4% -> 6% of each run, Pallas kernels for 0% -> 0%
where the time goes in v1:
time: 272 us; the launch traced here: 270 us
  other arithmetic  214 us (79%)
  waiting for transfers between devices  28.1 us (10%)
  starting transfers between devices  20.6 us (8%)
  matrix products  5.79 us (2%)
    dot_general x1, other arithmetic, local(): lax.dot_general(field_flat, image_flat, (((0,), (0,)), ((), ())), preferr...  185 us
    ppermute x4, waiting for transfers between devices, local(): lax.ppermute(summed, 'bricks', [(dev, dev ^ hop) for dev in range(16)])  25.4 us
    convert_element_type x1, other arithmetic, local(): padded_field.astype(jnp.float32)  11.4 us
    ppermute x4, starting transfers between devices, local(): lax.ppermute(summed, 'bricks', [(dev, dev ^ hop) for dev in range(16)])  8.62 us
    ppermute x2, starting transfers between devices, with_halo(): lax.ppermute(lax.slice_in_dim(block, block.shape[dim] - width, None, axis...  8.18 us
    mul x1, other arithmetic, local(): field = snapshots * occupied[None, :, :, None]  8.04 us
    dot_general x1, matrix products, local(): lax.dot_general(field_flat, image_flat, (((0,), (0,)), ((), ())), preferr...  5.79 us
  transfers between devices with their start and end apart: 8, of which 5 were waited for; matrix products, arithmetic and copies ran while one was open for 6% of the time, Pallas kernels for 0%

profile of v1, /device:TPU:1, one launch (start us, length us, event | category | flops | bytes accessed | tf_op | source)
XLA Modules:
  0.0 270.4 jit_solution(253087648752746168)
XLA Ops:
  0.0 0.7 convert_reduce_fusion
  1.1 0.7 convert_element_type.49
  1.8 1.1 select_reduce_fusion
  2.9 0.1 convert_element_type.51
  3.1 4.5 %collective-permute-start = (bf16[1,32,32]{2,1,0:T(8,128)(2,1)S(1)}, bf16[1,32,32]{2,1,0:T(8,128)(2,1)S(1)}, u32[]{:S(2)}, u32[]{:S(2)}) collective-permute-start(bf16[1,32,32]{2,1,0:T(8,128)(2,1)S(1)} %get-tuple-element.35), channel_id=1, source_target_pairs={{0,1},{1,2},{2,3},{3,4},{4,5},{5,6},{6,7},{7,8},{8,9},{9,10},{10,1... | collective-permute-start | bytes 6152 | tf_op jit(solution)/shard_map/ppermute | solution.py:12
  7.7 1.9 collective-permute-start.1
  9.6 8.0 %broadcast_multiply_fusion = bf16[16,32,32,256]{3,2,1,0:T(8,128)(2,1)} fusion(bf16[16,32,32,256]{3,2,1,0:T(8,128)(2,1)} %param.4, bf16[32,32]{1,0:T(8,128)(2,1)S(1)} %copy.11), kind=kLoop, calls=%fused_computation.30 | loop fusion | flops 4194304 | bytes 16779264 | tf_op jit(solution)/shard_map/mul | solution.py:68
  17.6 1.3 fusion.32
  18.9 3.6 %collective-permute-start.2 = (bf16[1,32,32,256]{3,2,1,0:T(8,128)(2,1)S(1)}, bf16[1,32,32,256]{3,2,1,0:T(8,128)(2,1)S(1)}, u32[]{:S(2)}, u32[]{:S(2)}) collective-permute-start(bf16[1,32,32,256]{3,2,1,0:T(8,128)(2,1)S(1)} %get-tuple-element.5), channel_id=1, source_target_pairs={{0,1},{1,2},{2,3},{3,4},{4,5},{5,6},{6,7},{7,8},{8,9},{9,10},{10,1... | collective-permute-start | bytes 1572872 | tf_op jit(solution)/shard_map/ppermute | solution.py:12
  22.6 1.9 collective-permute-start.3
  24.6 2.3 fusion.8
  26.9 3.5 %add_multiply_fusion = (f32[16,32,32]{2,1,0:T(8,128)S(1)}, f32[16,32,32]{2,1,0:T(8,128)S(1)}, f32[16,32,32]{2,1,0:T(8,128)S(1)}, f32[16,32,32]{2,1,0:T(8,128)S(1...) fusion(f32[18,32,32]{2,1,0:T(8,128)S(1)} %maximum_convert_fusion.1), kind=kLoop, calls=%fused_computation.78 | loop fusion | flops 966656 | bytes 2129920 | tf_op jit(solution)/shard_map/mul | solution.py:53
  30.4 2.7 collective-permute-done.3
  33.1 11.4 %maximum_convert_fusion = f32[18,32,32,256]{3,2,1,0:T(8,128)} fusion(bf16[1,32,32,256]{3,2,1,0:T(8,128)(2,1)S(1)} %collective-permute-done.3, bf16[16,32,32,256]{3,2,1,0:T(8,128)(2,1)} %broadcast_multiply_fusion, bf16[1,32,32,256]{3,2,1,0:T(8,128)(2,1)S(1)} %collective-permute-done.2), kind=kLoop, calls=%fused_computation.28 | loop fusion | flops 14155776 | bytes 28311552 | tf_op jit(solution)/shard_map/convert_element_type | solution.py:73
  44.4 185.4 %fusion.38 = bf16[16,32,32,256]{3,2,1,0:T(8,128)(2,1)S(1)} fusion(f32[18,32,32,256]{3,2,1,0:T(8,128)} %maximum_convert_fusion, f32[16,32,32]{2,1,0:T(8,128)} %get-tuple-element.32, f32[16,32,32]{2,1,0:T(8,128)} %get-tuple-element.31, f32[16,32,32]{2,1,0:T(8,128)} %get-tuple-element.30, f32[16,32,32]{2,1,0:T(8,128)} %get-tuple-element.29, ...), kind=kLoop, calls=%fused_computation.27.clone.clone.clone.clone.1 | loop fusion | flops 427819008 | bytes 83951616 | tf_op jit(solution)/shard_map/dot_general | solution.py:80
  229.8 5.8 %fusion.5 = f32[256,256]{1,0:T(8,128)S(1)} fusion(bf16[16,32,32,256]{3,2,1,0:T(8,128)(2,1)} %broadcast_multiply_fusion, bf16[16,32,32,256]{3,2,1,0:T(8,128)(2,1)S(1)} %fusion.38), kind=kOutput, calls=%fused_computation.31 | convolution fusion | flops 2147483648 | bytes 17039360 | tf_op jit(solution)/shard_map/dot_general | solution.py:80
  235.7 1.5 collective-permute-done.4
  237.2 3.2 %collective-permute-start.5 = (f32[256,256]{1,0:T(8,128)S(1)}, f32[256,256]{1,0:T(8,128)S(1)}, u32[]{:S(2)}, u32[]{:S(2)}) collective-permute-start(f32[256,256]{1,0:T(8,128)S(1)} %add.323), channel_id=1, source_target_pairs={{0,2},{1,3},{2,0},{3,1},{4,6},{5,7},{6,4},{7,5},{8,10},{9,11},{10,... | collective-permute-start | bytes 786440 | tf_op jit(solution)/shard_map/ppermute | solution.py:85
  240.4 6.5 %collective-permute-done.5 = f32[256,256]{1,0:T(8,128)S(1)} collective-permute-done((f32[256,256]{1,0:T(8,128)S(1)}, f32[256,256]{1,0:T(8,128)S(1)}, u32[]{:S(2)}, u32[]{:S(2)}) %collective-permute-start.5) | collective-permute-done | bytes 262176 | tf_op jit(solution)/shard_map/ppermute | solution.py:85
  247.0 3.1 %collective-permute-start.6 = (f32[256,256]{1,0:T(8,128)S(1)}, f32[256,256]{1,0:T(8,128)S(1)}, u32[]{:S(2)}, u32[]{:S(2)}) collective-permute-start(f32[256,256]{1,0:T(8,128)S(1)} %add.324), channel_id=1, source_target_pairs={{0,4},{1,5},{2,6},{3,7},{4,0},{5,1},{6,2},{7,3},{8,12},{9,13},{10,... | collective-permute-start | bytes 786440 | tf_op jit(solution)/shard_map/ppermute | solution.py:85
  250.2 5.7 %collective-permute-done.6 = f32[256,256]{1,0:T(8,128)S(1)} collective-permute-done((f32[256,256]{1,0:T(8,128)S(1)}, f32[256,256]{1,0:T(8,128)S(1)}, u32[]{:S(2)}, u32[]{:S(2)}) %collective-permute-start.6) | collective-permute-done | bytes 262176 | tf_op jit(solution)/shard_map/ppermute | solution.py:85
  255.9 2.2 collective-permute-start.7
  258.1 11.7 %collective-permute-done.7 = f32[256,256]{1,0:T(8,128)S(1)} collective-permute-done((f32[256,256]{1,0:T(8,128)S(1)}, f32[256,256]{1,0:T(8,128)S(1)}, u32[]{:S(2)}, u32[]{:S(2)}) %collective-permute-start.7) | collective-permute-done | bytes 262176 | tf_op jit(solution)/shard_map/ppermute | solution.py:85
  269.8 0.6 fusion.28
  (16 shorter events, 0.7 us)
Async XLA Ops:
  3.1 21.4 %collective-permute-start = (bf16[1,32,32]{2,1,0:T(8,128)(2,1)S(1)}, bf16[1,32,32]{2,1,0:T(8,128)(2,1)S(1)}, u32[]{:S(2)}, u32[]{:S(2)}) collective-permute-start(bf16[1,32,32]{2,1,0:T(8,128)(2,1)S(1)} %get-tuple-element.35), channel_id=1, source_target_pairs={{0,1},{1,2},{2,3},{3,4},{4,5},{5,6},{6,7},{7,8},{8,9},{9,10},{10,1... | collective-permute-start | bytes 6152 | tf_op jit(solution)/shard_map/ppermute | solution.py:12
  7.7 16.8 %collective-permute-start.1 = (bf16[1,32,32]{2,1,0:T(8,128)(2,1)S(1)}, bf16[1,32,32]{2,1,0:T(8,128)(2,1)S(1)}, u32[]{:S(2)}, u32[]{:S(2)}) collective-permute-start(bf16[1,32,32]{2,1,0:T(8,128)(2,1)S(1)} %get-tuple-element.36), channel_id=1, source_target_pairs={{1,0},{2,1},{3,2},{4,3},{5,4},{6,5},{7,6},{8,7},{9,8},{10,9},{11,1... | collective-permute-start | bytes 6152 | tf_op jit(solution)/shard_map/ppermute | solution.py:15
  18.9 11.5 %collective-permute-start.2 = (bf16[1,32,32,256]{3,2,1,0:T(8,128)(2,1)S(1)}, bf16[1,32,32,256]{3,2,1,0:T(8,128)(2,1)S(1)}, u32[]{:S(2)}, u32[]{:S(2)}) collective-permute-start(bf16[1,32,32,256]{3,2,1,0:T(8,128)(2,1)S(1)} %get-tuple-element.5), channel_id=1, source_target_pairs={{0,1},{1,2},{2,3},{3,4},{4,5},{5,6},{6,7},{7,8},{8,9},{9,10},{10,1... | collective-permute-start | bytes 1572872 | tf_op jit(solution)/shard_map/ppermute | solution.py:12
  22.6 10.5 %collective-permute-start.3 = (bf16[1,32,32,256]{3,2,1,0:T(8,128)(2,1)S(1)}, bf16[1,32,32,256]{3,2,1,0:T(8,128)(2,1)S(1)}, u32[]{:S(2)}, u32[]{:S(2)}) collective-permute-start(bf16[1,32,32,256]{3,2,1,0:T(8,128)(2,1)S(1)} %get-tuple-element.6), channel_id=1, source_target_pairs={{1,0},{2,1},{3,2},{4,3},{5,4},{6,5},{7,6},{8,7},{9,8},{10,9},{11,1... | collective-permute-start | bytes 1572872 | tf_op jit(solution)/shard_map/ppermute | solution.py:15
  235.6 1.6 collective-permute-start.4
  237.2 9.7 %collective-permute-start.5 = (f32[256,256]{1,0:T(8,128)S(1)}, f32[256,256]{1,0:T(8,128)S(1)}, u32[]{:S(2)}, u32[]{:S(2)}) collective-permute-start(f32[256,256]{1,0:T(8,128)S(1)} %add.323), channel_id=1, source_target_pairs={{0,2},{1,3},{2,0},{3,1},{4,6},{5,7},{6,4},{7,5},{8,10},{9,11},{10,... | collective-permute-start | bytes 786440 | tf_op jit(solution)/shard_map/ppermute | solution.py:85
  247.0 8.9 %collective-permute-start.6 = (f32[256,256]{1,0:T(8,128)S(1)}, f32[256,256]{1,0:T(8,128)S(1)}, u32[]{:S(2)}, u32[]{:S(2)}) collective-permute-start(f32[256,256]{1,0:T(8,128)S(1)} %add.324), channel_id=1, source_target_pairs={{0,4},{1,5},{2,6},{3,7},{4,0},{5,1},{6,2},{7,3},{8,12},{9,13},{10,... | collective-permute-start | bytes 786440 | tf_op jit(solution)/shard_map/ppermute | solution.py:85
  255.9 13.9 %collective-permute-start.7 = (f32[256,256]{1,0:T(8,128)S(1)}, f32[256,256]{1,0:T(8,128)S(1)}, u32[]{:S(2)}, u32[]{:S(2)}) collective-permute-start(f32[256,256]{1,0:T(8,128)S(1)} %add.325), channel_id=1, source_target_pairs={{0,8},{1,9},{2,10},{3,11},{4,12},{5,13},{6,14},{7,15},{8,0},{9,1},... | collective-permute-start | bytes 786440 | tf_op jit(solution)/shard_map/ppermute | solution.py:85
